TPU v7x, 32 devices: a whole 2x2x4 slice. The times are simulated.
32 devices in a mesh: grp: 2 (over core), blk: 16 (over z, y, x).
Axes of the slice: x: 2, y: 2, z: 4, core: 2. Of those that a mesh axis runs over, the one named last changes fastest.
Arguments:
- src_feats: bfloat16 [2, 4096, 512], P('grp', 'blk')
- tgt_feats: bfloat16 [2, 4096, 512], P('grp', 'blk')
- proj_weight: bfloat16 [512, 512], replicated, may hold values from -0.25 to 0.25
- match_blocks: int32 [2, 32, 4], P('grp', 'blk'), may hold values from 0 to 31, as said below
- match_count: int32 [2, 32], P('grp', 'blk'), may hold values from 1 to 4
- pair_src: int32 [2, 32, 4, 128], P('grp', 'blk'), may hold values from 0 to 127
- pair_tgt: int32 [2, 32, 4, 128], P('grp', 'blk'), may hold values from 0 to 127
Outputs:
- weight_grad: float32 [512, 512], replicated
- covariance: float32 [2, 512, 512], P('grp')
Inputs may be any that keep to these rules, and one draw needn't show every extreme that they name: `match_blocks`: each row lists 4 different target blocks; for source block s each listed block t has t // 2 at most 1 away from s // 2 along the loop of 16 runs (taken mod 16); unused slots follow the same rule.
All inputs are finite; a program needn't handle non-finite values.
Results may differ from a plain program's by a relative error of at most 0.0052.
Values may be sent and summed in bfloat16 or wider, within the bound.
No kernel may reach another device: no remote copies, remote signals or barrier semaphores. Data moves between devices by JAX's collectives and lax.ppermute only.
A program may use at most 64 MiB of HBM per device.

v0:
```python
import jax
import jax.numpy as jnp
from jax import lax
from jax.sharding import PartitionSpec as P

sharpness_divisor = 0.4
logit_bound = 2.5
norm_eps = 1e-06


def from_behind(shard, axis, by):
    count = lax.axis_size(axis)
    return lax.ppermute(shard, axis, [(i, (i + by) % count) for i in range(count)])


def project(features, weight_mat):
    projected = jnp.dot(features, weight_mat, preferred_element_type=jnp.float32)
    inv_norm = lax.rsqrt(jnp.sum(projected * projected, axis=1, keepdims=True) + norm_eps)
    unit_rows = projected * inv_norm
    return (unit_rows, inv_norm, unit_rows.astype(jnp.bfloat16))


def back_norm(unit_rows, inv_norm, grad_rows):
    inner = jnp.sum(unit_rows * grad_rows, axis=1, keepdims=True)
    return ((grad_rows - unit_rows * inner) * inv_norm).astype(jnp.bfloat16)


def pair_weights(anchor_stack, candidate_stack, onehot, matched):
    similarity_table = (
        jnp.einsum(
            "smd,skd->smk", anchor_stack, candidate_stack, preferred_element_type=jnp.float32
        )
        / sharpness_divisor
    )
    exp_terms = jnp.exp(similarity_table - logit_bound)
    shares = exp_terms / jnp.sum(exp_terms, axis=2, keepdims=True)
    linear_weights = (shares - onehot).astype(jnp.bfloat16)
    return linear_weights * matched.astype(jnp.bfloat16)[:, None, None]


def spread_blocks(target_total, linear_weights, anchor_stack, local_blocks, blocks_dev):
    slot_pieces = (
        jnp.einsum("smk,smd->skd", linear_weights, anchor_stack, preferred_element_type=jnp.float32)
        / sharpness_divisor
    )
    choice_mask = (
        local_blocks[:, None] == jnp.arange(blocks_dev, dtype=jnp.int32)[None, :]
    ).astype(jnp.float32)
    return target_total + jnp.einsum(
        "qm,qoi->moi", choice_mask, slot_pieces, precision=lax.Precision.HIGHEST
    )


def body(src_feats, tgt_feats, proj_weight, match_blocks, match_count, pair_src, pair_tgt):
    src_rows = src_feats[0]
    tgt_rows = tgt_feats[0]
    src_unit, source_inverse_norm, src_half = project(src_rows, proj_weight)
    tgt_unit, tgt_inv, tgt_half = project(tgt_rows, proj_weight)
    local_points = src_rows.shape[0]
    feature_width = src_rows.shape[1]
    blocks_dev = match_blocks.shape[1]
    slot_count = match_blocks.shape[2]
    matched_pair_count = pair_src.shape[3]
    block_points = local_points // blocks_dev
    slot_total = blocks_dev * slot_count
    runs = lax.axis_size("blk")
    reach_runs = runs // 16
    owning_run_index = lax.axis_index("blk")
    src_blocks = src_half.reshape(blocks_dev, block_points, feature_width)
    tgt_blocks = tgt_half.reshape(blocks_dev, block_points, feature_width)
    slot_index = jnp.arange(slot_count, dtype=jnp.int32)
    listed_flat = match_blocks[0].reshape(-1)
    live_flat = (slot_index[None, :] < match_count[0][:, None]).reshape(-1)
    block_base = (jnp.arange(blocks_dev, dtype=jnp.int32) * block_points)[:, None, None]
    row_index = (block_base + pair_src[0]).reshape(-1)
    tgt_table = pair_tgt[0].reshape(slot_total, matched_pair_count)
    query_stack = jnp.take(src_half, row_index, axis=0).reshape(
        slot_total, matched_pair_count, feature_width
    )
    columns = jnp.arange(block_points, dtype=jnp.int32)
    source_onehot = (tgt_table[:, :, None] == columns[None, None, :]).astype(jnp.float32)
    local_listed = listed_flat % blocks_dev
    query_zeros = jnp.zeros((slot_total * matched_pair_count, feature_width), jnp.float32)
    block_zeros = jnp.zeros((blocks_dev, block_points, feature_width), jnp.float32)

    def source_slots(held_tgt, run_id, query_total, target_total):
        matched = (listed_flat // blocks_dev == run_id) & live_flat
        candidate_stack = jnp.take(held_tgt, local_listed, axis=0)
        linear_weights = pair_weights(query_stack, candidate_stack, source_onehot, matched)
        query_part = (
            jnp.einsum(
                "smk,skd->smd", linear_weights, candidate_stack, preferred_element_type=jnp.float32
            )
            / sharpness_divisor
        )
        query_total = query_total + query_part.reshape(
            slot_total * matched_pair_count, feature_width
        )
        return (query_total, target_total)

    pair_table = jnp.concatenate(
        [pair_src[0].reshape(slot_total, matched_pair_count), tgt_table], axis=1
    )
    head_table = jnp.stack([listed_flat, live_flat.astype(jnp.int32)], axis=1)
    owner_base = (jnp.arange(slot_total, dtype=jnp.int32) // slot_count * block_points)[:, None]

    def target_slots(kept_source_rows, pair_rows, list_heads, target_total):
        target_blocks = list_heads[:, 0]
        matched = (target_blocks // blocks_dev == owning_run_index) & (list_heads[:, 1] > 0)
        their_src = pair_rows[:, :matched_pair_count]
        their_tgt = pair_rows[:, matched_pair_count:]
        gather_rows = (owner_base + their_src).reshape(-1)
        anchor_stack = jnp.take(
            kept_source_rows.reshape(local_points, feature_width), gather_rows, axis=0
        ).reshape(slot_total, matched_pair_count, feature_width)
        local_blocks = target_blocks % blocks_dev
        candidate_stack = jnp.take(tgt_blocks, local_blocks, axis=0)
        onehot = (their_tgt[:, :, None] == columns[None, None, :]).astype(jnp.float32)
        linear_weights = pair_weights(anchor_stack, candidate_stack, onehot, matched)
        return spread_blocks(target_total, linear_weights, anchor_stack, local_blocks, blocks_dev)

    def visit_run(held, run_id, totals):
        held_pair, pair_rows, list_heads = held
        query_total, target_total = totals
        query_total, _ = source_slots(held_pair[1], run_id, query_total, block_zeros)
        target_total = target_slots(held_pair[0], pair_rows, list_heads, target_total)
        return (query_total, target_total)

    own_held = (jnp.stack([src_blocks, tgt_blocks]), pair_table, head_table)
    totals = visit_run(own_held, owning_run_index, (query_zeros, block_zeros))

    def advance(offset, loop_state):
        ahead_held, behind_held, running = loop_state
        ahead_held = from_behind((ahead_held[0], ahead_held[1], ahead_held[2]), "blk", 1)
        behind_held = from_behind((behind_held[0], behind_held[1], behind_held[2]), "blk", -1)
        running = visit_run(ahead_held, (owning_run_index - offset) % runs, running)
        running = visit_run(behind_held, (owning_run_index + offset) % runs, running)
        return (ahead_held, behind_held, running)

    _, _, (anchor_loss_slope, grad_target) = lax.fori_loop(
        1, reach_runs + 1, advance, (own_held, own_held, totals)
    )
    grad_source = jax.ops.segment_sum(anchor_loss_slope, row_index, num_segments=local_points)
    src_grad = back_norm(src_unit, source_inverse_norm, grad_source)
    tgt_grad = back_norm(tgt_unit, tgt_inv, grad_target.reshape(local_points, feature_width))
    weight_part = lax.dot_general(
        src_rows, src_grad, (((0,), (0,)), ((), ())), preferred_element_type=jnp.float32
    )
    weight_part = weight_part + lax.dot_general(
        tgt_rows, tgt_grad, (((0,), (0,)), ((), ())), preferred_element_type=jnp.float32
    )
    weight_grad = lax.psum(weight_part, ("grp", "blk"))
    moment = lax.dot_general(
        src_half, src_half, (((0,), (0,)), ((), ())), preferred_element_type=jnp.float32
    )
    moment = moment + lax.dot_general(
        tgt_half, tgt_half, (((0,), (0,)), ((), ())), preferred_element_type=jnp.float32
    )
    moment = moment * (feature_width / (2.0 * local_points * runs))
    covariance = lax.psum(moment, "blk")
    return (weight_grad, covariance[None])


def solution(mesh):
    placed = (
        P("grp", "blk", None),
        P("grp", "blk", None),
        P(),
        P("grp", "blk", None),
        P("grp", "blk"),
        P("grp", "blk", None, None),
        P("grp", "blk", None, None),
    )
    return jax.shard_map(
        body, mesh=mesh, in_specs=placed, out_specs=(P(), P("grp", None, None)), check_vma=False
    )
```

profile of v0, /device:TPU:0, one launch (start us, length us, event | category | flops | bytes accessed | tf_op | source)
XLA Modules:
  0.0 379.4 jit_solution(14157346822565561980)
XLA Ops:
  7.2 0.0 all-reduce.3.cloned.1.call-start
  7.2 0.8 reshape_squeeze.10
  8.0 0.7 fusion.129
  8.8 0.1 reshape.340
  8.9 7.0 %collective-permute-start.4 = (s32[8,2]{0,1:T(2,128)S(1)}, s32[8,2]{0,1:T(2,128)S(1)}, u32[]{:S(2)}, u32[]{:S(2)}) collective-permute-start(s32[8,2]{0,1:T(2,128)S(1)} %pad_add_fusion.1), channel_id=1, source_target_pairs={{0,15},{1,0},{2,1},{3,2},{4,3},{5,4},{6,5},{7,6},{8,7},{9,8},{10,9... | collective-permute-start | bytes 200 | tf_op jit(solution)/shard_map/while/body/eval_jaxpr/ppermute | solution.py:13
  15.9 0.7 pad_add_fusion
  16.6 5.6 %collective-permute-start.5 = (s32[8,256]{1,0:T(8,128)S(1)}, s32[8,256]{1,0:T(8,128)S(1)}, u32[]{:S(2)}, u32[]{:S(2)}) collective-permute-start(s32[8,256]{1,0:T(8,128)S(1)} %pad_add_fusion), channel_id=1, source_target_pairs={{0,15},{1,0},{2,1},{3,2},{4,3},{5,4},{6,5},{7,6},{8,7},{9,8},{10,9... | collective-permute-start | bytes 24584 | tf_op jit(solution)/shard_map/while/body/eval_jaxpr/ppermute | solution.py:13
  22.2 1.3 multiply_reduce_fusion.2
  23.6 1.3 multiply_reduce_fusion.1
  24.9 0.1 multiply_convert_fusion.2
  25.0 0.1 multiply_convert_fusion.1
  25.1 0.9 pad_maximum_fusion
  26.0 5.6 %collective-permute-start.1 = (bf16[2,2,128,512]{3,2,1,0:T(8,128)(2,1)}, bf16[2,2,128,512]{3,2,1,0:T(8,128)(2,1)}, u32[]{:S(2)}, u32[]{:S(2)}) collective-permute-start(bf16[2,2,128,512]{3,2,1,0:T(8,128)(2,1)} %pad_maximum_fusion), channel_id=1, source_target_pairs={{0,15},{1,0},{2,1},{3,2},{4,3},{5,4},{6,5},{7,6},{8,7},{9,8},{10,9... | collective-permute-start | bytes 1572872 | tf_op jit(solution)/shard_map/while/body/eval_jaxpr/ppermute | solution.py:13
  31.6 0.1 reshape_squeeze.9
  31.7 0.1 lt.91
  31.8 0.1 add.197
  31.9 1.6 gather_fusion.1
  33.6 1.6 gather_fusion.8
  35.2 1.6 gather_fusion.6
  36.9 0.1 fusion.95
  36.9 4.0 %gather_fusion.4 = bf16[1024,512]{1,0:T(8,128)(2,1)S(1)} fusion(bf16[256,512]{1,0:T(8,128)(2,1)S(1)} %multiply_convert_fusion.2, s32[1024]{0:T(1024)S(1)} %get-tuple-element.77), kind=kCustom, calls=%fused_computation.2.clone | custom fusion | bytes 2101248 | tf_op jit(solution)/shard_map/jit(_take)/gather | solution.py:113
  40.9 5.1 %gather_fusion = bf16[1024,512]{1,0:T(8,128)(2,1)} fusion(bf16[256,512]{1,0:T(8,128)(2,1)S(1)} %multiply_convert_fusion.2, s32[1024]{0:T(1024)S(1)} %get-tuple-element.78), kind=kCustom, calls=%fused_computation.clone | custom fusion | bytes 2101248 | tf_op jit(solution)/shard_map/jit(_take)/gather | solution.py:77
  46.0 0.1 compare_and_fusion.2
  46.1 2.7 broadcast_select_fusion.5
  48.8 1.3 fusion.32
  50.1 0.5 copy-done.6
  50.6 3.1 fusion.52
  53.7 2.5 fusion.38
  56.2 3.3 convolution_multiply_fusion.2
  59.5 1.1 fusion.130
  60.6 5.1 %gather_fusion.5 = bf16[1024,512]{1,0:T(8,128)(2,1)} fusion(bf16[256,512]{1,0:T(8,128)(2,1)S(1)} %bitcast.154, s32[1024]{0:T(1024)S(1)} %get-tuple-element.86), kind=kCustom, calls=%fused_computation.3.clone | custom fusion | bytes 2101248 | tf_op jit(solution)/shard_map/while/body/eval_jaxpr/jit(_take)/gather | solution.py:113
  65.7 2.4 broadcast_select_fusion.4
  68.1 1.1 fusion.131
  69.1 5.1 %gather_fusion.7 = bf16[1024,512]{1,0:T(8,128)(2,1)} fusion(bf16[256,512]{1,0:T(8,128)(2,1)S(1)} %bitcast.153, s32[1024]{0:T(1024)S(1)} %get-tuple-element.87), kind=kCustom, calls=%fused_computation.4.clone | custom fusion | bytes 2101248 | tf_op jit(solution)/shard_map/while/body/eval_jaxpr/jit(_take)/gather | solution.py:113
  74.2 1.5 broadcast_select_fusion.3
  75.8 0.5 fusion.42
  76.3 0.4 copy-done.9
  76.7 3.1 convolution_multiply_fusion
  79.8 3.9 %fusion.6 = f32[2,128,512]{2,0,1:T(2,128)S(1)} fusion(f32[8,128,512]{2,1,0:T(8,128)} %convolution_multiply_fusion, s32[8]{0:T(128)S(1)} %fusion.117), kind=kOutput, calls=%fused_computation.16 | convolution fusion | flops 12582928 | bytes 2621472 | tf_op jit(solution)/shard_map/while/body/eval_jaxpr/qm,qoi->moi/dot_general | solution.py:49
  83.7 1.3 fusion.40
  85.0 3.3 convolution_multiply_fusion.1
  88.4 3.9 %fusion.8 = f32[2,128,512]{2,0,1:T(2,128)S(1)} fusion(f32[8,128,512]{2,1,0:T(8,128)} %convolution_multiply_fusion.1, s32[8]{0:T(128)S(1)} %fusion.116), kind=kOutput, calls=%fused_computation.18 | convolution fusion | flops 12582928 | bytes 2621472 | tf_op jit(solution)/shard_map/while/body/eval_jaxpr/qm,qoi->moi/dot_general | solution.py:49
  92.3 2.5 fusion.24
  94.8 0.1 copy.15
  94.9 0.2 fusion.61
  95.1 0.2 fusion.63
  95.3 1.6 gather_fusion.2
  96.9 2.8 fusion.34
  99.7 1.6 gather_fusion.3
  101.3 2.0 fusion.36
  103.3 3.5 fusion.50
  106.8 4.2 %add_multiply_fusion = f32[8,128,512]{2,1,0:T(8,128)} fusion(f32[8,128,512]{2,1,0:T(8,128)} %fusion.52, f32[8,128,512]{2,1,0:T(8,128)} %fusion.50, f32[8,128,128]{1,2,0:T(8,128)S(1)} %fusion.36, bf16[8,128,512]{2,1,0:T(8,128)(2,1)S(1)} %copy-done.1, pred[8]{0:T(512)(128)(4,1)S(1)} %get-tuple-element.90, s32[8,128]{1,0:T(8,128)S(1)} %bitcast.180, ...), kind=kOutput, calls=%fused_computation.22 | convolution fusion | flops 137495680 | bytes 7868440 | tf_op jit(solution)/shard_map/while/body/eval_jaxpr/smk,skd->smd/dot_general | solution.py:91
  111.0 7.6 %scatter_custom_fusion = f32[256,512]{1,0:T(8,128)S(1)} fusion(s32[1024]{0:T(1024)S(1)} %bitcast.181, f32[1024,512]{1,0:T(8,128)} %bitcast.159, f32[]{:T(128)} %constant.155.clone.1), kind=kCustom, calls=%fused_computation.124 | custom fusion | flops 524288 | bytes 524800 | tf_op jit(solution)/shard_map/scatter-add | solution.py:143
  118.6 0.2 multiply_reduce_fusion
  118.8 1.4 fusion.66
  120.2 1.3 fusion.14
  121.5 0.0 all-reduce.3.cloned.1.call-update
  121.5 0.0 all-reduce.5.cloned.1.call-start
  121.6 0.3 fusion.132
  121.9 1.3 fusion.13
  123.3 130.5 %all-reduce.3.cloned.1.call-done = f32[512,512]{0,1:T(8,128)} async-done(((f32[512,512]{0,1:T(8,128)}), f32[512,512]{0,1:T(8,128)}) %all-reduce.3.cloned.1.call-update) | async-done | bytes 1048592 | tf_op jit(solution)/shard_map/psum | solution.py:152
  253.7 2.5 copy.16
  256.3 114.1 %all-reduce.5.cloned.1.call-done = f32[1,512,512]{2,1,0:T(8,128)} async-done(((f32[1,512,512]{2,1,0:T(8,128)}), f32[1,512,512]{2,1,0:T(8,128)}) %all-reduce.5.cloned.1.call-update) | async-done | bytes 1048592 | tf_op jit(solution)/shard_map/psum | solution.py:160
  370.3 2.3 copy.32
  (60 shorter events, 0.3 us)
Async XLA Ops:
  7.2 15.0 %copy-start = (bf16[512,512]{1,0:T(8,128)(2,1)S(1)}, bf16[512,512]{1,0:T(8,128)(2,1)}, u32[]{:S(2)}) copy-start(bf16[512,512]{1,0:T(8,128)(2,1)} %param.13) | copy-start | bytes 1572868
  7.2 246.5 %all-reduce.3.cloned.1.call-start = ((), (), s32[]{:S(2)}) async-start(), calls=%async_computation | async-start | bytes 2097152 | tf_op jit(solution)/shard_map/psum | solution.py:152
  8.9 24.7 %collective-permute-start.4 = (s32[8,2]{0,1:T(2,128)S(1)}, s32[8,2]{0,1:T(2,128)S(1)}, u32[]{:S(2)}, u32[]{:S(2)}) collective-permute-start(s32[8,2]{0,1:T(2,128)S(1)} %pad_add_fusion.1), channel_id=1, source_target_pairs={{0,15},{1,0},{2,1},{3,2},{4,3},{5,4},{6,5},{7,6},{8,7},{9,8},{10,9... | collective-permute-start | bytes 200 | tf_op jit(solution)/shard_map/while/body/eval_jaxpr/ppermute | solution.py:13
  15.9 17.7 %collective-permute-start.2 = (s32[8,2]{0,1:T(2,128)S(1)}, s32[8,2]{0,1:T(2,128)S(1)}, u32[]{:S(2)}, u32[]{:S(2)}) collective-permute-start(s32[8,2]{0,1:T(2,128)S(1)} %pad_add_fusion.1), channel_id=1, source_target_pairs={{0,1},{1,2},{2,3},{3,4},{4,5},{5,6},{6,7},{7,8},{8,9},{9,10},{10,1... | collective-permute-start | bytes 200 | tf_op jit(solution)/shard_map/while/body/eval_jaxpr/ppermute | solution.py:13
  16.6 20.3 %collective-permute-start.5 = (s32[8,256]{1,0:T(8,128)S(1)}, s32[8,256]{1,0:T(8,128)S(1)}, u32[]{:S(2)}, u32[]{:S(2)}) collective-permute-start(s32[8,256]{1,0:T(8,128)S(1)} %pad_add_fusion), channel_id=1, source_target_pairs={{0,15},{1,0},{2,1},{3,2},{4,3},{5,4},{6,5},{7,6},{8,7},{9,8},{10,9... | collective-permute-start | bytes 24584 | tf_op jit(solution)/shard_map/while/body/eval_jaxpr/ppermute | solution.py:13
  22.2 14.7 %collective-permute-start.3 = (s32[8,256]{1,0:T(8,128)S(1)}, s32[8,256]{1,0:T(8,128)S(1)}, u32[]{:S(2)}, u32[]{:S(2)}) collective-permute-start(s32[8,256]{1,0:T(8,128)S(1)} %pad_add_fusion), channel_id=1, source_target_pairs={{0,1},{1,2},{2,3},{3,4},{4,5},{5,6},{6,7},{7,8},{8,9},{9,10},{10,1... | collective-permute-start | bytes 24584 | tf_op jit(solution)/shard_map/while/body/eval_jaxpr/ppermute | solution.py:13
  23.5 8.1 %copy-start.15 = (s32[1,2,4]{2,1,0:T(2,128)S(1)}, s32[1,2,4]{2,1,0:T(2,128)}, u32[]{:S(2)}) copy-start(s32[1,2,4]{2,1,0:T(2,128)} %param.14) | copy-start | bytes 100
  23.5 8.4 %copy-start.11 = (s32[1,2,4,128]{3,2,1,0:T(4,128)S(1)}, s32[1,2,4,128]{3,2,1,0:T(4,128)}, u32[]{:S(2)}) copy-start(s32[1,2,4,128]{3,2,1,0:T(4,128)} %param.16) | copy-start | bytes 12292
  26.0 42.1 %collective-permute-start.1 = (bf16[2,2,128,512]{3,2,1,0:T(8,128)(2,1)}, bf16[2,2,128,512]{3,2,1,0:T(8,128)(2,1)}, u32[]{:S(2)}, u32[]{:S(2)}) collective-permute-start(bf16[2,2,128,512]{3,2,1,0:T(8,128)(2,1)} %pad_maximum_fusion), channel_id=1, source_target_pairs={{0,15},{1,0},{2,1},{3,2},{4,3},{5,4},{6,5},{7,6},{8,7},{9,8},{10,9... | collective-permute-start | bytes 1572872 | tf_op jit(solution)/shard_map/while/body/eval_jaxpr/ppermute | solution.py:13
  33.5 26.0 %collective-permute-start = (bf16[2,2,128,512]{3,2,1,0:T(8,128)(2,1)}, bf16[2,2,128,512]{3,2,1,0:T(8,128)(2,1)}, u32[]{:S(2)}, u32[]{:S(2)}) collective-permute-start(bf16[2,2,128,512]{3,2,1,0:T(8,128)(2,1)} %pad_maximum_fusion), channel_id=1, source_target_pairs={{0,1},{1,2},{2,3},{3,4},{4,5},{5,6},{6,7},{7,8},{8,9},{9,10},{10,1... | collective-permute-start | bytes 1572872 | tf_op jit(solution)/shard_map/while/body/eval_jaxpr/ppermute | solution.py:13
  36.9 22.7 %copy-start.12 = (s32[8,256]{1,0:T(8,128)}, s32[8,256]{1,0:T(8,128)S(1)}, u32[]{:S(2)}) copy-start(s32[8,256]{1,0:T(8,128)S(1)} %collective-permute-done.5) | copy-start | bytes 24580
  36.9 22.7 %copy-start.13 = (s32[8,256]{1,0:T(8,128)}, s32[8,256]{1,0:T(8,128)S(1)}, u32[]{:S(2)}) copy-start(s32[8,256]{1,0:T(8,128)S(1)} %collective-permute-done.3) | copy-start | bytes 24580
  46.1 2.7 copy-start.5
  48.8 1.3 copy-start.10
  48.8 1.8 copy-start.6
  48.8 1.8 copy-start.14
  74.2 1.5 copy-start.4
  75.7 1.0 copy-start.9
  75.8 1.0 slice-start
  79.8 3.9 %copy-start.3 = (bf16[8,128,512]{2,1,0:T(8,128)(2,1)S(1)}, bf16[8,128,512]{2,1,0:T(8,128)(2,1)}, u32[]{:S(2)}) copy-start(bf16[8,128,512]{2,1,0:T(8,128)(2,1)} %gather_fusion.6) | copy-start | bytes 3145732
  79.8 3.9 %copy-start.8 = (bf16[1024,512]{1,0:T(8,128)(2,1)S(1)}, bf16[1024,512]{1,0:T(8,128)(2,1)}, u32[]{:S(2)}) copy-start(bf16[1024,512]{1,0:T(8,128)(2,1)} %broadcast_select_fusion.4) | copy-start | bytes 3145732
  83.7 1.3 slice-start.1
  88.4 3.9 %copy-start.2 = (f32[8,128,512]{2,1,0:T(8,128)S(1)}, f32[8,128,512]{2,1,0:T(8,128)}, u32[]{:S(2)}) copy-start(f32[8,128,512]{2,1,0:T(8,128)} %convolution_multiply_fusion.2) | copy-start | bytes 6291460
  103.3 3.5 copy-start.1
  111.0 9.2 %copy-start.7 = (bf16[1,256,512]{2,1,0:T(8,128)(2,1)S(1)}, bf16[1,256,512]{2,1,0:T(8,128)(2,1)}, u32[]{:S(2)}) copy-start(bf16[1,256,512]{2,1,0:T(8,128)(2,1)} %param.12) | copy-start | bytes 786436
  121.5 248.8 %all-reduce.5.cloned.1.call-start = ((), (), s32[]{:S(2)}) async-start(), calls=%async_computation.1 | async-start | bytes 2097152 | tf_op jit(solution)/shard_map/psum | solution.py:160
Sparse Core Ops, SparseCore 0:
  121.7 132.0 all-reduce.2
  259.0 111.2 all-reduce.4
where the time goes:
time: 380 us; the launch traced here: 379 us
  waiting for transfers between devices  245 us (64%)
  matrix products  48.3 us (13%)
  local copies, waits for them, and re-layouts  36.3 us (10%)
  starting transfers between devices  18.3 us (5%)
  other arithmetic  17.5 us (5%)
  between operations  14.4 us (4%)
    psum x1, waiting for transfers between devices, body(): weight_grad = lax.psum(weight_part, ('grp', 'blk'))  130 us
    psum x1, waiting for transfers between devices, body(): covariance = lax.psum(moment, 'blk')  114 us
    ppermute x6, starting transfers between devices, from_behind(): lax.ppermute(shard, axis, [(i, (i + by) % count) for i in range(count)])  18.2 us
    gather x3, local copies, waits for them, and re-layouts, target_slots(): jnp.take(kept_source_rows.reshape(local_points, feature_width), gather_ro...  14.1 us
    dot_general x3, matrix products, source_slots(): jnp.einsum('smk,skd->smd', linear_weights, candidate_stack, preferred_ele...  10.8 us
    dot_general x6, matrix products, pair_weights(): jnp.einsum('smd,skd->smk', anchor_stack, candidate_stack, preferred_eleme...  10.5 us
    dot_general x3, matrix products, spread_blocks(): jnp.einsum('qm,qoi->moi', choice_mask, slot_pieces, precision=lax.Precisi...  10.3 us
    dot_general x3, matrix products, spread_blocks(): jnp.einsum('smk,smd->skd', linear_weights, anchor_stack, preferred_elemen...  9.73 us
  transfers between devices with their start and end apart: 8, of which 2 were waited for; matrix products, arithmetic and copies ran while one was open for 12% of the time, Pallas kernels for 0%

commit v1 on v0

--- a/solution.py
+++ b/solution.py
@@ -149,7 +149,7 @@
     weight_part = weight_part + lax.dot_general(
         tgt_rows, tgt_grad, (((0,), (0,)), ((), ())), preferred_element_type=jnp.float32
     )
-    weight_grad = lax.psum(weight_part, ("grp", "blk"))
+    weight_grad = lax.psum(lax.psum(weight_part, "blk"), "grp")
     moment = lax.dot_general(
         src_half, src_half, (((0,), (0,)), ((), ())), preferred_element_type=jnp.float32
     )

time: 380 us -> 275 us (0.72)
  waiting for transfers between devices: 245 us -> 149 us
  local copies, waits for them, and re-layouts: 36.3 us -> 30.9 us
    psum x2, waiting for transfers between devices: 245 us -> 149 us  [body(): weight_grad = lax.psum(lax.psum(weight_part, 'blk'), 'grp')]
  transfers between devices with their start and end apart: 8 -> 8, of which waited for: 2 -> 2; matrix products, arithmetic and copies ran while one was open for 12% -> 14% of each run, Pallas kernels for 0% -> 0%
where the time goes in v1:
time: 275 us; the launch traced here: 274 us
  waiting for transfers between devices  149 us (54%)
  matrix products  45.9 us (17%)
  local copies, waits for them, and re-layouts  30.9 us (11%)
  starting transfers between devices  18.3 us (7%)
  other arithmetic  15 us (5%)
  between operations  14.4 us (5%)
    psum x2, waiting for transfers between devices, body(): weight_grad = lax.psum(lax.psum(weight_part, 'blk'), 'grp')  149 us
    ppermute x6, starting transfers between devices, from_behind(): lax.ppermute(shard, axis, [(i, (i + by) % count) for i in range(count)])  18.2 us
    gather x3, local copies, waits for them, and re-layouts, target_slots(): jnp.take(kept_source_rows.reshape(local_points, feature_width), gather_ro...  12.1 us
    dot_general x3, matrix products, source_slots(): jnp.einsum('smk,skd->smd', linear_weights, candidate_stack, preferred_ele...  10.8 us
    dot_general x3, matrix products, spread_blocks(): jnp.einsum('qm,qoi->moi', choice_mask, slot_pieces, precision=lax.Precisi...  10.3 us
    dot_general x3, matrix products, spread_blocks(): jnp.einsum('smk,smd->skd', linear_weights, anchor_stack, preferred_elemen...  9.42 us
    dot_general x6, matrix products, pair_weights(): jnp.einsum('smd,skd->smk', anchor_stack, candidate_stack, preferred_eleme...  9.42 us
    scatter-add x1, other arithmetic, body(): jax.ops.segment_sum(anchor_loss_slope, row_index, num_segments=local_points)  7.6 us
  transfers between devices with their start and end apart: 8, of which 2 were waited for; matrix products, arithmetic and copies ran while one was open for 14% of the time, Pallas kernels for 0%

profile of v1, /device:TPU:0, one launch (start us, length us, event | category | flops | bytes accessed | tf_op | source)
XLA Modules:
  0.0 273.8 jit_solution(10170104762988953560)
XLA Ops:
  7.2 0.0 all-reduce.6.cloned.1.call-start
  7.2 0.8 reshape_squeeze.10
  8.0 0.7 fusion.129
  8.8 0.1 reshape.340
  8.9 7.0 %collective-permute-start.4 = (s32[8,2]{0,1:T(2,128)S(1)}, s32[8,2]{0,1:T(2,128)S(1)}, u32[]{:S(2)}, u32[]{:S(2)}) collective-permute-start(s32[8,2]{0,1:T(2,128)S(1)} %pad_add_fusion.1), channel_id=1, source_target_pairs={{0,15},{1,0},{2,1},{3,2},{4,3},{5,4},{6,5},{7,6},{8,7},{9,8},{10,9... | collective-permute-start | bytes 200 | tf_op jit(solution)/shard_map/while/body/eval_jaxpr/ppermute | solution.py:13
  15.9 0.7 pad_add_fusion
  16.6 5.6 %collective-permute-start.5 = (s32[8,256]{1,0:T(8,128)S(1)}, s32[8,256]{1,0:T(8,128)S(1)}, u32[]{:S(2)}, u32[]{:S(2)}) collective-permute-start(s32[8,256]{1,0:T(8,128)S(1)} %pad_add_fusion), channel_id=1, source_target_pairs={{0,15},{1,0},{2,1},{3,2},{4,3},{5,4},{6,5},{7,6},{8,7},{9,8},{10,9... | collective-permute-start | bytes 24584 | tf_op jit(solution)/shard_map/while/body/eval_jaxpr/ppermute | solution.py:13
  22.2 1.3 multiply_reduce_fusion.2
  23.5 1.3 multiply_reduce_fusion.1
  24.9 0.1 multiply_convert_fusion.2
  25.0 0.1 multiply_convert_fusion.1
  25.1 0.9 pad_maximum_fusion
  26.0 5.6 %collective-permute-start.1 = (bf16[2,2,128,512]{3,2,1,0:T(8,128)(2,1)}, bf16[2,2,128,512]{3,2,1,0:T(8,128)(2,1)}, u32[]{:S(2)}, u32[]{:S(2)}) collective-permute-start(bf16[2,2,128,512]{3,2,1,0:T(8,128)(2,1)} %pad_maximum_fusion), channel_id=1, source_target_pairs={{0,15},{1,0},{2,1},{3,2},{4,3},{5,4},{6,5},{7,6},{8,7},{9,8},{10,9... | collective-permute-start | bytes 1572872 | tf_op jit(solution)/shard_map/while/body/eval_jaxpr/ppermute | solution.py:13
  31.6 0.1 reshape_squeeze.9
  31.7 0.3 fusion.132
  32.0 0.1 lt.91
  32.1 1.3 fusion.13
  33.5 0.1 add.199
  33.6 1.6 gather_fusion.1
  35.3 1.6 gather_fusion.8
  36.8 1.7 gather_fusion.6
  38.5 0.1 fusion.95
  38.6 4.0 %gather_fusion.4 = bf16[1024,512]{1,0:T(8,128)(2,1)S(1)} fusion(bf16[256,512]{1,0:T(8,128)(2,1)S(1)} %multiply_convert_fusion.2, s32[1024]{0:T(1024)S(1)} %get-tuple-element.79), kind=kCustom, calls=%fused_computation.2.clone | custom fusion | bytes 2101248 | tf_op jit(solution)/shard_map/jit(_take)/gather | solution.py:113
  42.6 5.1 %gather_fusion = bf16[1024,512]{1,0:T(8,128)(2,1)} fusion(bf16[256,512]{1,0:T(8,128)(2,1)S(1)} %multiply_convert_fusion.2, s32[1024]{0:T(1024)S(1)} %get-tuple-element.80), kind=kCustom, calls=%fused_computation.clone | custom fusion | bytes 2101248 | tf_op jit(solution)/shard_map/jit(_take)/gather | solution.py:77
  47.6 0.1 compare_and_fusion.2
  47.7 2.7 broadcast_select_fusion.5
  50.4 1.3 fusion.32
  51.7 0.5 copy-done.5
  52.2 3.1 %fusion.52 = f32[8,128,512]{2,1,0:T(8,128)} fusion(f32[8,128,128]{1,2,0:T(8,128)} %fusion.32, s32[8,128]{1,0:T(8,128)S(1)} %bitcast.177, bf16[8]{0:T(256)(128)(2,1)S(1)} %get-tuple-element.85, bf16[8,128,512]{2,1,0:T(8,128)(2,1)S(1)} %copy-done.5, pred[8]{0:T(512)(128)(4,1)S(1)} %get-tuple-element.92), kind=kOutput, calls=%fused_computation.70 | convolution fusion | flops 135922816 | bytes 3674136 | tf_op jit(solution)/shard_map/smk,skd->smd/dot_general | solution.py:91
  55.3 2.5 fusion.38
  57.8 3.3 %convolution_multiply_fusion.2 = f32[8,128,512]{2,1,0:T(8,128)} fusion(bf16[8,128,512]{2,1,0:T(8,128)(2,1)} %bitcast.168, f32[8,128,128]{1,2,0:T(8,128)} %fusion.38, s32[8,128]{1,0:T(8,128)S(1)} %bitcast.178, bf16[8]{0:T(256)(128)(2,1)S(1)} %get-tuple-element.46), kind=kOutput, calls=%fused_computation.25 | convolution fusion | flops 135922816 | bytes 3674128 | tf_op jit(solution)/shard_map/smk,smd->skd/dot_general | solution.py:43
  61.2 4.0 %gather_fusion.5 = bf16[1024,512]{1,0:T(8,128)(2,1)S(1)} fusion(bf16[256,512]{1,0:T(8,128)(2,1)S(1)} %bitcast.154, s32[1024]{0:T(1024)S(1)} %get-tuple-element.88), kind=kCustom, calls=%fused_computation.3.clone | custom fusion | bytes 2101248 | tf_op jit(solution)/shard_map/while/body/eval_jaxpr/jit(_take)/gather | solution.py:113
  65.2 1.2 broadcast_select_fusion.4
  66.4 1.1 fusion.131
  67.4 4.1 %gather_fusion.7 = bf16[1024,512]{1,0:T(8,128)(2,1)S(1)} fusion(bf16[256,512]{1,0:T(8,128)(2,1)S(1)} %bitcast.153, s32[1024]{0:T(1024)S(1)} %get-tuple-element.89), kind=kCustom, calls=%fused_computation.4.clone | custom fusion | bytes 2101248 | tf_op jit(solution)/shard_map/while/body/eval_jaxpr/jit(_take)/gather | solution.py:113
  71.6 0.2 broadcast_select_fusion.3
  71.8 1.2 copy-done.3
  73.0 0.5 fusion.42
  73.5 3.0 %convolution_multiply_fusion = f32[8,128,512]{2,1,0:T(8,128)} fusion(bf16[8,128,512]{2,1,0:T(8,128)(2,1)} %bitcast.163, f32[8,128,128]{1,2,0:T(8,128)S(1)} %fusion.42, s32[8,128]{1,0:T(8,128)S(1)} %slice-done, bf16[8]{0:T(256)(128)(2,1)S(1)} %get-tuple-element.82), kind=kOutput, calls=%fused_computation.23 | convolution fusion | flops 135922816 | bytes 3674128 | tf_op jit(solution)/shard_map/while/body/eval_jaxpr/smk,smd->skd/dot_general | solution.py:43
  76.6 3.9 %fusion.6 = f32[2,128,512]{2,0,1:T(2,128)S(1)} fusion(f32[8,128,512]{2,1,0:T(8,128)} %convolution_multiply_fusion, s32[8]{0:T(128)S(1)} %fusion.117), kind=kOutput, calls=%fused_computation.16 | convolution fusion | flops 12582928 | bytes 2621472 | tf_op jit(solution)/shard_map/while/body/eval_jaxpr/qm,qoi->moi/dot_general | solution.py:49
  80.5 0.5 fusion.40
  81.0 0.1 slice-done.1
  81.2 3.0 %convolution_multiply_fusion.1 = f32[8,128,512]{2,1,0:T(8,128)} fusion(bf16[8,128,512]{2,1,0:T(8,128)(2,1)} %bitcast.160, f32[8,128,128]{1,2,0:T(8,128)S(1)} %fusion.40, s32[8,128]{1,0:T(8,128)S(1)} %slice-done.1, bf16[8]{0:T(256)(128)(2,1)S(1)} %get-tuple-element.81), kind=kOutput, calls=%fused_computation.24 | convolution fusion | flops 135922816 | bytes 3674128 | tf_op jit(solution)/shard_map/while/body/eval_jaxpr/smk,smd->skd/dot_general | solution.py:43
  84.2 3.9 %fusion.8 = f32[2,128,512]{2,0,1:T(2,128)S(1)} fusion(f32[8,128,512]{2,1,0:T(8,128)} %convolution_multiply_fusion.1, s32[8]{0:T(128)S(1)} %fusion.116), kind=kOutput, calls=%fused_computation.18 | convolution fusion | flops 12582928 | bytes 2621472 | tf_op jit(solution)/shard_map/while/body/eval_jaxpr/qm,qoi->moi/dot_general | solution.py:49
  88.2 2.5 fusion.24
  90.6 0.1 copy.15
  90.8 0.2 fusion.61
  91.0 0.2 fusion.63
  91.1 0.6 gather_fusion.2
  91.8 2.9 %fusion.34 = f32[8,128,128]{1,2,0:T(8,128)} fusion(bf16[8,128,512]{2,1,0:T(8,128)(2,1)} %bitcast.165, bf16[8,128,512]{2,1,0:T(8,128)(2,1)S(1)} %gather_fusion.2, pred[8]{0:T(512)(128)(4,1)S(1)} %get-tuple-element.92), kind=kOutput, calls=%fused_computation.52 | convolution fusion | flops 135004160 | bytes 2621448 | tf_op jit(solution)/shard_map/while/body/eval_jaxpr/smd,skd->smk/dot_general | solution.py:30
  94.7 0.6 gather_fusion.3
  95.3 1.7 fusion.36
  97.0 3.4 %fusion.50 = f32[8,128,512]{2,1,0:T(8,128)} fusion(f32[8,128,128]{1,2,0:T(8,128)} %fusion.34, bf16[8,128,512]{2,1,0:T(8,128)(2,1)} %copy-done.6, pred[8]{0:T(512)(128)(4,1)S(1)} %get-tuple-element.92, s32[8,128]{1,0:T(8,128)S(1)} %bitcast.179, bf16[8]{0:T(256)(128)(2,1)S(1)} %get-tuple-element.84), kind=kOutput, calls=%fused_computation.68 | convolution fusion | flops 135922816 | bytes 3674136 | tf_op jit(solution)/shard_map/while/body/eval_jaxpr/smk,skd->smd/dot_general | solution.py:91
  100.4 4.2 %add_multiply_fusion = f32[8,128,512]{2,1,0:T(8,128)} fusion(f32[8,128,512]{2,1,0:T(8,128)} %fusion.52, f32[8,128,512]{2,1,0:T(8,128)} %fusion.50, f32[8,128,128]{1,2,0:T(8,128)S(1)} %fusion.36, bf16[8,128,512]{2,1,0:T(8,128)(2,1)S(1)} %gather_fusion.3, pred[8]{0:T(512)(128)(4,1)S(1)} %get-tuple-element.92, s32[8,128]{1,0:T(8,128)S(1)} %bitcast.180, ...), kind=kOutput, calls=%fused_computation.22 | convolution fusion | flops 137495680 | bytes 7868440 | tf_op jit(solution)/shard_map/while/body/eval_jaxpr/smk,skd->smd/dot_general | solution.py:91
  104.7 7.6 %scatter_custom_fusion = f32[256,512]{1,0:T(8,128)S(1)} fusion(s32[1024]{0:T(1024)S(1)} %bitcast.181, f32[1024,512]{1,0:T(8,128)} %bitcast.159, f32[]{:T(128)} %constant.155.clone.1), kind=kCustom, calls=%fused_computation.124 | custom fusion | flops 524288 | bytes 524800 | tf_op jit(solution)/shard_map/scatter-add | solution.py:143
  112.3 0.2 multiply_reduce_fusion
  112.5 0.4 fusion.66
  112.9 1.3 fusion.14
  114.2 0.0 all-reduce.6.cloned.1.call-update
  114.2 0.0 all-reduce.4.cloned.1.call-start
  114.3 128.2 %all-reduce.6.cloned.1.call-done = (f32[512,512]{0,1:T(8,128)}, f32[1,512,512]{2,1,0:T(8,128)}) async-done(((f32[512,512]{0,1:T(8,128)}, f32[1,512,512]{2,1,0:T(8,128)}), (f32[512,512]{0,1:T(8,128)}, f32[1,512,512]{2,1,0:T(8,128)})) %all-reduce.6.cloned.1.call-update) | async-done | bytes 2097168 | tf_op jit(solution)/shard_map/psum | solution.py:152
  242.5 21.0 %all-reduce.4.cloned.1.call-done = f32[512,512]{0,1:T(8,128)} async-done(((f32[512,512]{0,1:T(8,128)}), f32[512,512]{0,1:T(8,128)}) %all-reduce.4.cloned.1.call-update) | async-done | bytes 1048592 | tf_op jit(solution)/shard_map/psum | solution.py:152
  263.5 2.5 copy.16
  266.0 1.0 copy.33
  (64 shorter events, 0.3 us)
Async XLA Ops:
  7.2 15.0 %copy-start = (bf16[512,512]{1,0:T(8,128)(2,1)S(1)}, bf16[512,512]{1,0:T(8,128)(2,1)}, u32[]{:S(2)}) copy-start(bf16[512,512]{1,0:T(8,128)(2,1)} %param.13) | copy-start | bytes 1572868
  7.2 235.3 %all-reduce.6.cloned.1.call-start = ((), (), s32[]{:S(2)}) async-start(), calls=%async_computation.1 | async-start | bytes 4194304 | tf_op jit(solution)/shard_map/psum | solution.py:152
  8.9 26.3 %collective-permute-start.4 = (s32[8,2]{0,1:T(2,128)S(1)}, s32[8,2]{0,1:T(2,128)S(1)}, u32[]{:S(2)}, u32[]{:S(2)}) collective-permute-start(s32[8,2]{0,1:T(2,128)S(1)} %pad_add_fusion.1), channel_id=1, source_target_pairs={{0,15},{1,0},{2,1},{3,2},{4,3},{5,4},{6,5},{7,6},{8,7},{9,8},{10,9... | collective-permute-start | bytes 200 | tf_op jit(solution)/shard_map/while/body/eval_jaxpr/ppermute | solution.py:13
  15.9 19.3 %collective-permute-start.2 = (s32[8,2]{0,1:T(2,128)S(1)}, s32[8,2]{0,1:T(2,128)S(1)}, u32[]{:S(2)}, u32[]{:S(2)}) collective-permute-start(s32[8,2]{0,1:T(2,128)S(1)} %pad_add_fusion.1), channel_id=1, source_target_pairs={{0,1},{1,2},{2,3},{3,4},{4,5},{5,6},{6,7},{7,8},{8,9},{9,10},{10,1... | collective-permute-start | bytes 200 | tf_op jit(solution)/shard_map/while/body/eval_jaxpr/ppermute | solution.py:13
  16.6 21.9 %collective-permute-start.5 = (s32[8,256]{1,0:T(8,128)S(1)}, s32[8,256]{1,0:T(8,128)S(1)}, u32[]{:S(2)}, u32[]{:S(2)}) collective-permute-start(s32[8,256]{1,0:T(8,128)S(1)} %pad_add_fusion), channel_id=1, source_target_pairs={{0,15},{1,0},{2,1},{3,2},{4,3},{5,4},{6,5},{7,6},{8,7},{9,8},{10,9... | collective-permute-start | bytes 24584 | tf_op jit(solution)/shard_map/while/body/eval_jaxpr/ppermute | solution.py:13
  22.2 16.3 %collective-permute-start.3 = (s32[8,256]{1,0:T(8,128)S(1)}, s32[8,256]{1,0:T(8,128)S(1)}, u32[]{:S(2)}, u32[]{:S(2)}) collective-permute-start(s32[8,256]{1,0:T(8,128)S(1)} %pad_add_fusion), channel_id=1, source_target_pairs={{0,1},{1,2},{2,3},{3,4},{4,5},{5,6},{6,7},{7,8},{8,9},{9,10},{10,1... | collective-permute-start | bytes 24584 | tf_op jit(solution)/shard_map/while/body/eval_jaxpr/ppermute | solution.py:13
  23.5 8.1 %copy-start.17 = (s32[1,2,4]{2,1,0:T(2,128)S(1)}, s32[1,2,4]{2,1,0:T(2,128)}, u32[]{:S(2)}) copy-start(s32[1,2,4]{2,1,0:T(2,128)} %param.14) | copy-start | bytes 100
  26.0 40.4 %collective-permute-start.1 = (bf16[2,2,128,512]{3,2,1,0:T(8,128)(2,1)}, bf16[2,2,128,512]{3,2,1,0:T(8,128)(2,1)}, u32[]{:S(2)}, u32[]{:S(2)}) collective-permute-start(bf16[2,2,128,512]{3,2,1,0:T(8,128)(2,1)} %pad_maximum_fusion), channel_id=1, source_target_pairs={{0,15},{1,0},{2,1},{3,2},{4,3},{5,4},{6,5},{7,6},{8,7},{9,8},{10,9... | collective-permute-start | bytes 1572872 | tf_op jit(solution)/shard_map/while/body/eval_jaxpr/ppermute | solution.py:13
  31.7 1.8 copy-start.13
  35.2 26.0 %collective-permute-start = (bf16[2,2,128,512]{3,2,1,0:T(8,128)(2,1)}, bf16[2,2,128,512]{3,2,1,0:T(8,128)(2,1)S(1)}, u32[]{:S(2)}, u32[]{:S(2)}) collective-permute-start(bf16[2,2,128,512]{3,2,1,0:T(8,128)(2,1)} %pad_maximum_fusion), channel_id=1, source_target_pairs={{0,1},{1,2},{2,3},{3,4},{4,5},{5,6},{6,7},{7,8},{8,9},{9,10},{10,1... | collective-permute-start | bytes 1572872 | tf_op jit(solution)/shard_map/while/body/eval_jaxpr/ppermute | solution.py:13
  38.5 22.7 %copy-start.14 = (s32[8,256]{1,0:T(8,128)}, s32[8,256]{1,0:T(8,128)S(1)}, u32[]{:S(2)}) copy-start(s32[8,256]{1,0:T(8,128)S(1)} %collective-permute-done.5) | copy-start | bytes 24580
  38.5 22.7 %copy-start.15 = (s32[8,256]{1,0:T(8,128)}, s32[8,256]{1,0:T(8,128)S(1)}, u32[]{:S(2)}) copy-start(s32[8,256]{1,0:T(8,128)S(1)} %collective-permute-done.3) | copy-start | bytes 24580
  47.7 2.7 copy-start.4
  50.4 1.3 copy-start.11
  50.4 1.8 copy-start.5
  50.4 1.8 copy-start.16
  71.6 1.4 copy-start.3
  71.8 1.7 copy-start.10
  71.8 1.7 slice-start
  76.6 3.9 %copy-start.2 = (bf16[8,128,512]{2,1,0:T(8,128)(2,1)S(1)}, bf16[8,128,512]{2,1,0:T(8,128)(2,1)}, u32[]{:S(2)}) copy-start(bf16[8,128,512]{2,1,0:T(8,128)(2,1)} %gather_fusion.6) | copy-start | bytes 3145732
  76.6 3.9 %copy-start.9 = (bf16[1024,512]{1,0:T(8,128)(2,1)S(1)}, bf16[1024,512]{1,0:T(8,128)(2,1)}, u32[]{:S(2)}) copy-start(bf16[1024,512]{1,0:T(8,128)(2,1)} %broadcast_select_fusion.4) | copy-start | bytes 3145732
  80.5 0.7 slice-start.1
  84.2 3.9 %copy-start.1 = (f32[8,128,512]{2,1,0:T(8,128)S(1)}, f32[8,128,512]{2,1,0:T(8,128)}, u32[]{:S(2)}) copy-start(f32[8,128,512]{2,1,0:T(8,128)} %convolution_multiply_fusion.2) | copy-start | bytes 6291460
  91.7 2.9 %copy-start.6 = (bf16[8,128,512]{2,1,0:T(8,128)(2,1)}, bf16[8,128,512]{2,1,0:T(8,128)(2,1)S(1)}, u32[]{:S(2)}) copy-start(bf16[8,128,512]{2,1,0:T(8,128)(2,1)S(1)} %gather_fusion.2) | copy-start | bytes 3145732
  100.4 12.0 %copy-start.12 = (bf16[1,256,512]{2,1,0:T(8,128)(2,1)S(1)}, bf16[1,256,512]{2,1,0:T(8,128)(2,1)}, u32[]{:S(2)}) copy-start(bf16[1,256,512]{2,1,0:T(8,128)(2,1)} %param.11) | copy-start | bytes 786436
  104.7 8.3 %copy-start.8 = (bf16[1,256,512]{2,1,0:T(8,128)(2,1)S(1)}, bf16[1,256,512]{2,1,0:T(8,128)(2,1)}, u32[]{:S(2)}) copy-start(bf16[1,256,512]{2,1,0:T(8,128)(2,1)} %param.12) | copy-start | bytes 786436
  114.2 149.3 %all-reduce.4.cloned.1.call-start = ((), (), s32[]{:S(2)}) async-start(), calls=%async_computation | async-start | bytes 2097152 | tf_op jit(solution)/shard_map/psum | solution.py:152
  242.5 23.6 %copy-start.7 = (f32[1,512,512]{2,1,0:T(8,128)S(1)}, f32[1,512,512]{2,1,0:T(8,128)}, u32[]{:S(2)}) copy-start(f32[1,512,512]{2,1,0:T(8,128)} %get-tuple-element.101) | copy-start | bytes 3145732
Sparse Core Ops, SparseCore 0:
  114.4 128.0 all-reduce.5
  244.8 18.6 all-reduce.3
